TPU v7x, 32 devices: a whole 2x2x4 slice. The times are simulated.
32 devices in a mesh: grp: 2 (over y), tile: 16 (over z, x, core).
Axes of the slice: x: 2, y: 2, z: 4, core: 2. Of those that a mesh axis runs over, the one named last changes fastest.
Arguments:
- rhs: float32 [256, 28672], P('grp', 'tile'), parts along dimension 0, may hold values from -4.5 to 4.5
- mass_diag: float32 [28672], P('tile'), may hold values from 0.1 to 2
- edge_heads: int32 [114688], P('tile'), may hold values from 128 to 1919
- edge_tails: int32 [114688], P('tile'), may hold values from 0 to 2047
- edge_weight: float32 [114688], P('tile'), may hold values from 0.5 to 2
- local_inverse: bfloat16 [32768, 2048], P('tile'), may hold values from -0.5 to 1
- coarse_vec: float32 [28672], P('tile'), may hold values from 0.25 to 1.75
- coarse_inv: float32 [16, 16], replicated, may hold values from -0.000558035714 to 0.002232143
Outputs:
- solution: float32 [256, 28672], P('grp', 'tile'), parts along dimension 0
- residual: float32 [256, 28672], P('grp', 'tile'), parts along dimension 0
There are 2 independent parts, one for each index of `grp`. A program takes and returns all parts, laid end to end along the dimension named above; an argument that names none is the same for every part. Nothing has to cross between parts.
All inputs are finite; a program needn't handle non-finite values.
Results may differ from a plain program's by a relative error of at most 0.015.
Values may be sent and summed in bfloat16 or wider, within the bound.
No kernel may reach another device: no remote copies, remote signals or barrier semaphores. Data moves between devices by JAX's collectives and lax.ppermute only.
A program may use at most 128 MiB of HBM per device.

v0:
```python
import jax
import jax.numpy as jnp
from jax import lax
from jax.sharding import PartitionSpec as P

SUB = 2048
STRIP = 128
ITERS = 2


def with_halo(block, sides, width):
    for axis, dim in sides:
        count = lax.axis_size(axis)
        forward = [(i, i + 1) for i in range(count - 1)]
        backward = [(target, source) for source, target in forward]
        low = lax.ppermute(
            lax.slice_in_dim(block, block.shape[dim] - width, None, axis=dim), axis, forward
        )
        high = lax.ppermute(lax.slice_in_dim(block, 0, width, axis=dim), axis, backward)
        block = jnp.concatenate([low, block, high], axis=dim)
    return block


def send_back(contrib):
    rims = jnp.concatenate([contrib[:, :STRIP], contrib[:, -STRIP:]], axis=1)
    arrived = with_halo(rims.astype(jnp.bfloat16), (("tile", 1),), STRIP).astype(rims.dtype)
    owned = contrib[:, STRIP:-STRIP]
    lower = owned[:, :STRIP] + arrived[:, :STRIP]
    upper = owned[:, -STRIP:] + arrived[:, -STRIP:]
    return jnp.concatenate([lower, owned[:, STRIP:-STRIP], upper], axis=1)


def build_stiffness(edge_heads, edge_tails, edge_weight):
    rows_idx = jnp.concatenate([edge_heads, edge_tails, edge_heads, edge_tails])
    cols_idx = jnp.concatenate([edge_heads, edge_tails, edge_tails, edge_heads])
    values = jnp.concatenate([edge_weight, edge_weight, -edge_weight, -edge_weight])
    return jnp.zeros((SUB, SUB), jnp.float32).at[rows_idx, cols_idx].add(values)


def operate(vector, mass_diag, stiffness):
    widened = with_halo(vector, (("tile", 1),), STRIP)
    contrib = jnp.dot(widened, stiffness, precision=lax.Precision.HIGHEST)
    return mass_diag * vector + send_back(contrib)


def precondition(resid, local_inverse, coarse_vec, coarse_inv):
    widened = with_halo(resid.astype(jnp.bfloat16), (("tile", 1),), STRIP)
    local = jnp.dot(widened, local_inverse, preferred_element_type=jnp.float32)
    schwarz = send_back(local)
    restricted = jnp.sum(resid * coarse_vec, axis=1)
    mine_index = lax.axis_index("tile")
    every = lax.all_gather(restricted[:, None], "tile", axis=1, tiled=True)
    column = lax.dynamic_slice_in_dim(coarse_inv, mine_index, 1, 1)
    mine = jnp.dot(every, column, precision=lax.Precision.HIGHEST)
    return schwarz + mine * coarse_vec


def inner(left, right):
    return jnp.sum(left * right, axis=1)


def both_dots(resid, zvec, image):
    return lax.psum((inner(resid, zvec), inner(image, zvec)), "tile")


def shards(
    rhs, mass_diag, edge_heads, edge_tails, edge_weight, local_inverse, coarse_vec, coarse_inv
):
    stiffness = build_stiffness(edge_heads, edge_tails, edge_weight)
    solution = jnp.zeros_like(rhs)
    resid = rhs
    zvec = precondition(resid, local_inverse, coarse_vec, coarse_inv)
    image = operate(zvec, mass_diag, stiffness)
    gamma, delta = both_dots(resid, zvec, image)
    alpha = gamma / delta
    direction, along = (zvec, image)
    for step in range(ITERS):
        solution = solution + alpha[:, None] * direction
        resid = resid - alpha[:, None] * along
        if step + 1 < ITERS:
            zvec = precondition(resid, local_inverse, coarse_vec, coarse_inv)
            image = operate(zvec, mass_diag, stiffness)
            gamma_next, delta = both_dots(resid, zvec, image)
            ratio = gamma_next / gamma
            alpha = gamma_next / (delta - ratio * gamma_next / alpha)
            direction = zvec + ratio[:, None] * direction
            along = image + ratio[:, None] * along
            gamma = gamma_next
    return (solution, resid)


def solution(mesh):
    return jax.shard_map(
        shards,
        mesh=mesh,
        in_specs=(
            P("grp", "tile"),
            P("tile"),
            P("tile"),
            P("tile"),
            P("tile"),
            P("tile", None),
            P("tile"),
            P(),
        ),
        out_specs=(P("grp", "tile"), P("grp", "tile")),
        check_vma=False,
    )
```

profile of v0, /device:TPU:0, one launch (start us, length us, event | category | flops | bytes accessed | tf_op | source)
XLA Modules:
  0.0 372.3 jit_solution(4083867110889075399)
XLA Ops:
  0.6 0.0 copy-start
  0.7 1.7 multiply_reduce_fusion.5
  2.4 1.3 collective-permute-start.1
  3.7 3.0 collective-permute-start
  6.7 1.1 compare_select_fusion.1
  7.8 0.5 and_reduce_fusion
  8.3 1.1 multiply_reduce_fusion.6
  9.4 0.2 dynamic-slice_reduce_fusion
  9.6 23.1 %all-gather = f32[16,1,128]{2,1,0:T(1,128)S(1)} all-gather(f32[1,1,128]{2,1,0:T(1,128)S(1)} %bitcast.29), channel_id=1, replica_groups=mesh['grp'=2,'tile'=16] {'tile'}, dimensions={0}, use_global_device_ids=true | all-gather | bytes 8704 | tf_op jit(solution)/shard_map/all_gather | solution.py:52
  32.7 0.0 collective-permute-done.1
  32.7 0.0 collective-permute-done
  32.7 4.7 %fusion.40 = (bf16[128,2048]{1,0:T(8,128)(2,1)S(1)}, f32[128,2048]{1,0:T(8,128)S(1)}) fusion(bf16[2048,2048]{1,0:T(8,128)(2,1)} %param.13, bf16[128,128]{1,0:T(8,128)(2,1)S(1)} %collective-permute-done.1, bf16[128,1792]{1,0:T(8,128)(2,1)S(1)} %get-tuple-element.29, bf16[128,128]{1,0:T(8,128)(2,1)S(1)} %collective-permute-done), kind=kOutput, calls=%fused_computation.86 | convolution fusion | flops 1075576832 | bytes 10485760 | tf_op jit(solution)/shard_map/dot_general | solution.py:48
  37.5 1.3 collective-permute-start.3
  38.8 3.0 collective-permute-start.2
  41.8 0.1 convolution_bitcast_fusion.1
  42.0 0.1 slice.181
  42.0 0.0 collective-permute-done.3
  42.1 0.6 collective-permute-done.2
  42.7 0.1 maximum_add_fusion
  42.9 1.3 collective-permute-start.5
  44.2 4.3 %collective-permute-start.4 = (f32[128,128]{1,0:T(8,128)S(1)}, f32[128,128]{1,0:T(8,128)S(1)}, u32[]{:S(2)}, u32[]{:S(2)}) collective-permute-start(f32[128,128]{1,0:T(8,128)S(1)} %get-tuple-element.26), channel_id=1, source_target_pairs={{0,1},{1,2},{2,3},{3,4},{4,5},{5,6},{6,7},{7,8},{8,9},{9,10},{10,1... | collective-permute-start | bytes 196616 | tf_op jit(solution)/shard_map/ppermute | solution.py:16
  48.5 156.5 %scatter_custom_fusion = f32[4194304]{0:T(1024)} fusion(s32[28672]{0:T(1024)S(1)} %broadcast_select_fusion, f32[28672]{0:T(1024)S(1)} %pad_maximum_fusion, f32[]{:T(128)} %constant.5.clone.1), kind=kCustom, calls=%fused_computation.1 | custom fusion | flops 28672 | bytes 16777220
  205.0 18.0 %reshape.335 = f32[2048,2048]{1,0:T(8,128)} reshape(f32[4194304]{0:T(1024)} %scatter_custom_fusion) | data formatting | bytes 33554432 | tf_op jit(solution)/shard_map/scatter-add | solution.py:37
  223.0 0.0 collective-permute-done.5
  223.0 0.0 collective-permute-done.4
  223.0 12.8 %fusion.41 = (bf16[128,2048]{1,0:T(8,128)(2,1)S(1)}, f32[128,2048]{1,0:T(8,128)S(1)}) fusion(f32[2048,2048]{1,0:T(8,128)} %reshape.335, f32[128,128]{1,0:T(8,128)S(1)} %collective-permute-done.5, f32[128,1792]{1,0:T(8,128)S(1)} %maximum_add_fusion, f32[128,128]{1,0:T(8,128)S(1)} %collective-permute-done.4), kind=kOutput, calls=%fused_computation.87 | convolution fusion | flops 6443237376 | bytes 19398656 | tf_op jit(solution)/shard_map/dot_general | solution.py:42
  235.8 1.3 collective-permute-start.7
  237.1 5.0 %collective-permute-start.6 = (bf16[128,128]{1,0:T(8,128)(2,1)S(1)}, bf16[128,128]{1,0:T(8,128)(2,1)S(1)}, u32[]{:S(2)}, u32[]{:S(2)}) collective-permute-start(bf16[128,128]{1,0:T(8,128)(2,1)S(1)} %get-tuple-element.34), channel_id=1, source_target_pairs={{0,1},{1,2},{2,3},{3,4},{4,5},{5,6},{6,7},{7,8},{8,9},{9,10},{10,1... | collective-permute-start | bytes 98312 | tf_op jit(solution)/shard_map/ppermute | solution.py:16
  242.2 0.1 slice.188
  242.2 0.6 collective-permute-done.6
  242.9 0.3 multiply_reduce_fusion.3
  243.2 31.4 %all-reduce.1 = (f32[128]{0:T(128)S(1)}, f32[128]{0:T(128)S(1)}) all-reduce(f32[128]{0:T(128)S(1)} %get-tuple-element.5, f32[128]{0:T(128)S(1)} %get-tuple-element.4), channel_id=1, replica_groups=mesh['grp'=2,'tile'=16] {'tile'}, use_global_device_ids=true, to_apply=%region_2.0 | all-reduce | flops 256 | bytes 2048 | tf_op jit(solution)/shard_map/psum | solution.py:63
  274.6 0.5 copy-done.13
  275.1 1.2 multiply_reduce_fusion.2
  276.4 1.3 collective-permute-start.9
  277.7 3.0 collective-permute-start.8
  280.7 17.1 %all-gather.1 = f32[16,1,128]{2,1,0:T(1,128)S(1)} all-gather(f32[1,1,128]{2,1,0:T(1,128)S(1)} %bitcast.30), channel_id=1, replica_groups=mesh['grp'=2,'tile'=16] {'tile'}, dimensions={0}, use_global_device_ids=true | all-gather | bytes 8704 | tf_op jit(solution)/shard_map/all_gather | solution.py:52
  297.8 0.0 collective-permute-done.8
  297.9 4.7 %fusion.42 = (bf16[128,2048]{1,0:T(8,128)(2,1)S(1)}, f32[128,2048]{1,0:T(8,128)S(1)}) fusion(bf16[2048,2048]{1,0:T(8,128)(2,1)} %param.13, bf16[128,128]{1,0:T(8,128)(2,1)S(1)} %collective-permute-done.9, bf16[128,1792]{1,0:T(8,128)(2,1)S(1)} %convert_element_type.25, bf16[128,128]{1,0:T(8,128)(2,1)S(1)} %collective-permute-done.8), kind=kOutput, calls=%fused_computation.88 | convolution fusion | flops 1075576832 | bytes 10485760 | tf_op jit(solution)/shard_map/dot_general | solution.py:48
  302.6 0.0 copy-start.9
  302.6 1.3 collective-permute-start.11
  303.9 3.0 collective-permute-start.10
  306.9 0.8 convolution_bitcast_fusion
  307.7 0.1 slice.195
  307.8 0.0 collective-permute-done.11
  307.8 0.0 collective-permute-done.10
  307.8 0.1 maximum_add_fusion.2
  308.0 1.3 collective-permute-start.13
  309.3 4.3 %collective-permute-start.12 = (f32[128,128]{1,0:T(8,128)S(1)}, f32[128,128]{1,0:T(8,128)S(1)}, u32[]{:S(2)}, u32[]{:S(2)}) collective-permute-start(f32[128,128]{1,0:T(8,128)S(1)} %get-tuple-element.24), channel_id=1, source_target_pairs={{0,1},{1,2},{2,3},{3,4},{4,5},{5,6},{6,7},{7,8},{8,9},{9,10},{10,1... | collective-permute-start | bytes 196616 | tf_op jit(solution)/shard_map/ppermute | solution.py:16
  313.6 0.0 collective-permute-done.13
  313.6 0.9 collective-permute-done.12
  314.5 12.7 %fusion.43 = (bf16[128,2048]{1,0:T(8,128)(2,1)S(1)}, f32[128,2048]{1,0:T(8,128)S(1)}) fusion(f32[2048,2048]{1,0:T(8,128)} %reshape.335, f32[128,128]{1,0:T(8,128)S(1)} %collective-permute-done.13, f32[128,1792]{1,0:T(8,128)S(1)} %maximum_add_fusion.2, f32[128,128]{1,0:T(8,128)S(1)} %collective-permute-done.12), kind=kOutput, calls=%fused_computation.89 | convolution fusion | flops 6443237376 | bytes 19398656 | tf_op jit(solution)/shard_map/dot_general | solution.py:42
  327.2 1.3 collective-permute-start.15
  328.5 5.9 %collective-permute-start.14 = (bf16[128,128]{1,0:T(8,128)(2,1)S(1)}, bf16[128,128]{1,0:T(8,128)(2,1)S(1)}, u32[]{:S(2)}, u32[]{:S(2)}) collective-permute-start(bf16[128,128]{1,0:T(8,128)(2,1)S(1)} %get-tuple-element.30), channel_id=1, source_target_pairs={{0,1},{1,2},{2,3},{3,4},{4,5},{5,6},{6,7},{7,8},{8,9},{9,10},{10,1... | collective-permute-start | bytes 98312 | tf_op jit(solution)/shard_map/ppermute | solution.py:16
  334.4 0.1 slice.202
  334.4 0.0 collective-permute-done.15
  334.5 0.8 collective-permute-done.14
  335.3 0.1 copy-done.2
  335.3 0.3 multiply_reduce_fusion
  335.6 0.2 copy-done.5
  335.9 0.0 copy-done.6
  335.9 32.6 %all-reduce = (f32[128]{0:T(128)}, f32[128]{0:T(128)}) all-reduce(f32[128]{0:T(128)S(1)} %get-tuple-element.3, f32[128]{0:T(128)S(1)} %get-tuple-element.2), channel_id=1, replica_groups=mesh['grp'=2,'tile'=16] {'tile'}, use_global_device_ids=true, to_apply=%region_8.0 | all-reduce | flops 256 | bytes 2048 | tf_op jit(solution)/shard_map/psum | solution.py:63
  368.5 0.7 subtract_divide_fusion
  369.2 3.1 multiply_subtract_fusion
  (43 shorter events, 0.3 us)
Async XLA Ops:
  0.6 8.8 %copy-start = (f32[16,16]{1,0:T(8,128)S(1)}, f32[16,16]{1,0:T(8,128)}, u32[]{:S(2)}) copy-start(f32[16,16]{1,0:T(8,128)} %param.15) | copy-start | bytes 3076
  0.6 42.1 %copy-start.7 = (f32[1792]{0:T(1024)S(1)}, f32[1792]{0:T(1024)}, u32[]{:S(2)}) copy-start(f32[1792]{0:T(1024)} %param.14) | copy-start | bytes 21508
  0.7 41.3 %copy-start.10 = (f32[7168]{0:T(1024)S(1)}, f32[7168]{0:T(1024)}, u32[]{:S(2)}) copy-start(f32[7168]{0:T(1024)} %param.12) | copy-start | bytes 86020
  2.4 30.4 %collective-permute-start.1 = (bf16[128,128]{1,0:T(8,128)(2,1)S(1)}, bf16[128,128]{1,0:T(8,128)(2,1)S(1)}, u32[]{:S(2)}, u32[]{:S(2)}) collective-permute-start(bf16[128,128]{1,0:T(8,128)(2,1)S(1)} %get-tuple-element.41), channel_id=1, source_target_pairs={{1,0},{2,1},{3,2},{4,3},{5,4},{6,5},{7,6},{8,7},{9,8},{10,9},{11,1... | collective-permute-start | bytes 98312 | tf_op jit(solution)/shard_map/ppermute | solution.py:19
  3.7 29.1 %collective-permute-start = (bf16[128,128]{1,0:T(8,128)(2,1)S(1)}, bf16[128,128]{1,0:T(8,128)(2,1)S(1)}, u32[]{:S(2)}, u32[]{:S(2)}) collective-permute-start(bf16[128,128]{1,0:T(8,128)(2,1)S(1)} %get-tuple-element.40), channel_id=1, source_target_pairs={{0,1},{1,2},{2,3},{3,4},{4,5},{5,6},{6,7},{7,8},{8,9},{9,10},{10,1... | collective-permute-start | bytes 98312 | tf_op jit(solution)/shard_map/ppermute | solution.py:16
  9.6 33.1 %copy-start.11 = (f32[16]{0:T(128)}, f32[16]{0:T(128)S(1)}, u32[]{:S(2)}) copy-start(f32[16]{0:T(128)S(1)} %dynamic-slice_reduce_fusion) | copy-start | bytes 196
  37.5 4.6 %collective-permute-start.3 = (bf16[128,128]{1,0:T(8,128)(2,1)S(1)}, bf16[128,128]{1,0:T(8,128)(2,1)S(1)}, u32[]{:S(2)}, u32[]{:S(2)}) collective-permute-start(bf16[128,128]{1,0:T(8,128)(2,1)S(1)} %get-tuple-element.37), channel_id=1, source_target_pairs={{1,0},{2,1},{3,2},{4,3},{5,4},{6,5},{7,6},{8,7},{9,8},{10,9},{11,1... | collective-permute-start | bytes 98312 | tf_op jit(solution)/shard_map/ppermute | solution.py:19
  38.8 3.9 %collective-permute-start.2 = (bf16[128,128]{1,0:T(8,128)(2,1)S(1)}, bf16[128,128]{1,0:T(8,128)(2,1)S(1)}, u32[]{:S(2)}, u32[]{:S(2)}) collective-permute-start(bf16[128,128]{1,0:T(8,128)(2,1)S(1)} %get-tuple-element.36), channel_id=1, source_target_pairs={{0,1},{1,2},{2,3},{3,4},{4,5},{5,6},{6,7},{7,8},{8,9},{9,10},{10,1... | collective-permute-start | bytes 98312 | tf_op jit(solution)/shard_map/ppermute | solution.py:16
  42.9 180.1 %collective-permute-start.5 = (f32[128,128]{1,0:T(8,128)S(1)}, f32[128,128]{1,0:T(8,128)S(1)}, u32[]{:S(2)}, u32[]{:S(2)}) collective-permute-start(f32[128,128]{1,0:T(8,128)S(1)} %get-tuple-element.27), channel_id=1, source_target_pairs={{1,0},{2,1},{3,2},{4,3},{5,4},{6,5},{7,6},{8,7},{9,8},{10,9},{11,1... | collective-permute-start | bytes 196616 | tf_op jit(solution)/shard_map/ppermute | solution.py:19
  44.2 178.8 %collective-permute-start.4 = (f32[128,128]{1,0:T(8,128)S(1)}, f32[128,128]{1,0:T(8,128)S(1)}, u32[]{:S(2)}, u32[]{:S(2)}) collective-permute-start(f32[128,128]{1,0:T(8,128)S(1)} %get-tuple-element.26), channel_id=1, source_target_pairs={{0,1},{1,2},{2,3},{3,4},{4,5},{5,6},{6,7},{7,8},{8,9},{9,10},{10,1... | collective-permute-start | bytes 196616 | tf_op jit(solution)/shard_map/ppermute | solution.py:16
  223.0 19.9 %copy-start.1 = (f32[128,1792]{1,0:T(8,128)S(1)}, f32[128,1792]{1,0:T(8,128)}, u32[]{:S(2)}) copy-start(f32[128,1792]{1,0:T(8,128)} %param.8) | copy-start | bytes 2752516
  223.0 19.9 %copy-start.8 = (f32[1792]{0:T(1024)S(1)}, f32[1792]{0:T(1024)}, u32[]{:S(2)}) copy-start(f32[1792]{0:T(1024)} %param.9) | copy-start | bytes 21508
  235.8 6.4 %collective-permute-start.7 = (bf16[128,128]{1,0:T(8,128)(2,1)S(1)}, bf16[128,128]{1,0:T(8,128)(2,1)S(1)}, u32[]{:S(2)}, u32[]{:S(2)}) collective-permute-start(bf16[128,128]{1,0:T(8,128)(2,1)S(1)} %get-tuple-element.35), channel_id=1, source_target_pairs={{1,0},{2,1},{3,2},{4,3},{5,4},{6,5},{7,6},{8,7},{9,8},{10,9},{11,1... | collective-permute-start | bytes 98312 | tf_op jit(solution)/shard_map/ppermute | solution.py:19
  237.1 5.7 %collective-permute-start.6 = (bf16[128,128]{1,0:T(8,128)(2,1)S(1)}, bf16[128,128]{1,0:T(8,128)(2,1)S(1)}, u32[]{:S(2)}, u32[]{:S(2)}) collective-permute-start(bf16[128,128]{1,0:T(8,128)(2,1)S(1)} %get-tuple-element.34), channel_id=1, source_target_pairs={{0,1},{1,2},{2,3},{3,4},{4,5},{5,6},{6,7},{7,8},{8,9},{9,10},{10,1... | collective-permute-start | bytes 98312 | tf_op jit(solution)/shard_map/ppermute | solution.py:16
  242.8 31.7 %copy-start.3 = (f32[128,128]{1,0:T(8,128)}, f32[128,128]{1,0:T(8,128)S(1)}, u32[]{:S(2)}) copy-start(f32[128,128]{1,0:T(8,128)S(1)} %get-tuple-element.20) | copy-start | bytes 196612
  242.8 31.7 %copy-start.4 = (f32[128,128]{1,0:T(8,128)}, f32[128,128]{1,0:T(8,128)S(1)}, u32[]{:S(2)}) copy-start(f32[128,128]{1,0:T(8,128)S(1)} %get-tuple-element.21) | copy-start | bytes 196612
  274.5 0.5 copy-start.13
  274.5 0.5 copy-start.14
  275.1 22.8 %copy-start.12 = (f32[128]{0:T(128)}, f32[128]{0:T(128)S(1)}, u32[]{:S(2)}) copy-start(f32[128]{0:T(128)S(1)} %div.12) | copy-start | bytes 1540
  276.4 21.5 %collective-permute-start.9 = (bf16[128,128]{1,0:T(8,128)(2,1)S(1)}, bf16[128,128]{1,0:T(8,128)(2,1)S(1)}, u32[]{:S(2)}, u32[]{:S(2)}) collective-permute-start(bf16[128,128]{1,0:T(8,128)(2,1)S(1)} %get-tuple-element.39), channel_id=1, source_target_pairs={{1,0},{2,1},{3,2},{4,3},{5,4},{6,5},{7,6},{8,7},{9,8},{10,9},{11,1... | collective-permute-start | bytes 98312 | tf_op jit(solution)/shard_map/ppermute | solution.py:19
  277.7 20.2 %collective-permute-start.8 = (bf16[128,128]{1,0:T(8,128)(2,1)S(1)}, bf16[128,128]{1,0:T(8,128)(2,1)S(1)}, u32[]{:S(2)}, u32[]{:S(2)}) collective-permute-start(bf16[128,128]{1,0:T(8,128)(2,1)S(1)} %get-tuple-element.38), channel_id=1, source_target_pairs={{0,1},{1,2},{2,3},{3,4},{4,5},{5,6},{6,7},{7,8},{8,9},{9,10},{10,1... | collective-permute-start | bytes 98312 | tf_op jit(solution)/shard_map/ppermute | solution.py:16
  302.6 32.8 %copy-start.9 = (f32[1792]{0:T(1024)S(1)}, f32[1792]{0:T(1024)}, u32[]{:S(2)}) copy-start(f32[1792]{0:T(1024)} %param.9) | copy-start | bytes 21508
  302.6 5.2 %collective-permute-start.11 = (bf16[128,128]{1,0:T(8,128)(2,1)S(1)}, bf16[128,128]{1,0:T(8,128)(2,1)S(1)}, u32[]{:S(2)}, u32[]{:S(2)}) collective-permute-start(bf16[128,128]{1,0:T(8,128)(2,1)S(1)} %get-tuple-element.33), channel_id=1, source_target_pairs={{1,0},{2,1},{3,2},{4,3},{5,4},{6,5},{7,6},{8,7},{9,8},{10,9},{11,1... | collective-permute-start | bytes 98312 | tf_op jit(solution)/shard_map/ppermute | solution.py:19
  303.9 3.9 %collective-permute-start.10 = (bf16[128,128]{1,0:T(8,128)(2,1)S(1)}, bf16[128,128]{1,0:T(8,128)(2,1)S(1)}, u32[]{:S(2)}, u32[]{:S(2)}) collective-permute-start(bf16[128,128]{1,0:T(8,128)(2,1)S(1)} %get-tuple-element.32), channel_id=1, source_target_pairs={{0,1},{1,2},{2,3},{3,4},{4,5},{5,6},{6,7},{7,8},{8,9},{9,10},{10,1... | collective-permute-start | bytes 98312 | tf_op jit(solution)/shard_map/ppermute | solution.py:16
  308.0 5.6 %collective-permute-start.13 = (f32[128,128]{1,0:T(8,128)S(1)}, f32[128,128]{1,0:T(8,128)S(1)}, u32[]{:S(2)}, u32[]{:S(2)}) collective-permute-start(f32[128,128]{1,0:T(8,128)S(1)} %get-tuple-element.25), channel_id=1, source_target_pairs={{1,0},{2,1},{3,2},{4,3},{5,4},{6,5},{7,6},{8,7},{9,8},{10,9},{11,1... | collective-permute-start | bytes 196616 | tf_op jit(solution)/shard_map/ppermute | solution.py:19
  309.3 5.2 %collective-permute-start.12 = (f32[128,128]{1,0:T(8,128)S(1)}, f32[128,128]{1,0:T(8,128)S(1)}, u32[]{:S(2)}, u32[]{:S(2)}) collective-permute-start(f32[128,128]{1,0:T(8,128)S(1)} %get-tuple-element.24), channel_id=1, source_target_pairs={{0,1},{1,2},{2,3},{3,4},{4,5},{5,6},{6,7},{7,8},{8,9},{9,10},{10,1... | collective-permute-start | bytes 196616 | tf_op jit(solution)/shard_map/ppermute | solution.py:16
  327.2 7.2 %collective-permute-start.15 = (bf16[128,128]{1,0:T(8,128)(2,1)S(1)}, bf16[128,128]{1,0:T(8,128)(2,1)S(1)}, u32[]{:S(2)}, u32[]{:S(2)}) collective-permute-start(bf16[128,128]{1,0:T(8,128)(2,1)S(1)} %get-tuple-element.31), channel_id=1, source_target_pairs={{1,0},{2,1},{3,2},{4,3},{5,4},{6,5},{7,6},{8,7},{9,8},{10,9},{11,1... | collective-permute-start | bytes 98312 | tf_op jit(solution)/shard_map/ppermute | solution.py:19
  328.5 6.7 %collective-permute-start.14 = (bf16[128,128]{1,0:T(8,128)(2,1)S(1)}, bf16[128,128]{1,0:T(8,128)(2,1)S(1)}, u32[]{:S(2)}, u32[]{:S(2)}) collective-permute-start(bf16[128,128]{1,0:T(8,128)(2,1)S(1)} %get-tuple-element.30), channel_id=1, source_target_pairs={{0,1},{1,2},{2,3},{3,4},{4,5},{5,6},{6,7},{7,8},{8,9},{9,10},{10,1... | collective-permute-start | bytes 98312 | tf_op jit(solution)/shard_map/ppermute | solution.py:16
  334.4 0.9 copy-start.2
  335.2 0.6 copy-start.5
  335.2 0.7 copy-start.6
where the time goes:
time: 374 us; the launch traced here: 372 us
  other arithmetic  167 us (45%)
  blocking collectives  104 us (28%)
  starting transfers between devices  41.9 us (11%)
  matrix products  35.9 us (10%)
  local copies, waits for them, and re-layouts  19.4 us (5%)
    unnamed x4, other arithmetic  158 us
    psum x2, blocking collectives, both_dots(): return lax.psum((inner(resid, zvec), inner(image, zvec)), 'tile')  64 us
    all_gather x2, blocking collectives, precondition(): every = lax.all_gather(restricted[:, None], 'tile', axis=1, tiled=True)  40.3 us
    ppermute x8, starting transfers between devices, with_halo(): lax.ppermute(lax.slice_in_dim(block, block.shape[dim] - width, None, axis...  31.6 us
    dot_general x2, matrix products, operate(): contrib = jnp.dot(widened, stiffness, precision=lax.Precision.HIGHEST)  25.5 us
    scatter-add x1, local copies, waits for them, and re-layouts, build_stiffness(): return jnp.zeros((SUB, SUB), jnp.float32).at[rows_idx, cols_idx].add(values)  18 us
    ppermute x8, starting transfers between devices, with_halo(): lax.ppermute(lax.slice_in_dim(block, 0, width, axis=dim), axis, backward)  10.3 us
    dot_general x2, matrix products, precondition(): local = jnp.dot(widened, local_inverse, preferred_element_type=jnp.float32)  9.43 us
  transfers between devices with their start and end apart: 16, of which 4 were waited for; matrix products, arithmetic and copies ran while one was open for 48% of the time, Pallas kernels for 0%

commit v1 on v0

--- a/solution.py
+++ b/solution.py
@@ -49,7 +49,24 @@
     schwarz = send_back(local)
     restricted = jnp.sum(resid * coarse_vec, axis=1)
     mine_index = lax.axis_index("tile")
-    every = lax.all_gather(restricted[:, None], "tile", axis=1, tiled=True)
+    shard = restricted[:, None]
+    ways, here, step_2 = (lax.axis_size("tile"), lax.axis_index("tile"), shard.shape[1])
+    shape = [n * ways if d == 1 else n for d, n in enumerate(shard.shape)]
+    full = lax.dynamic_update_slice_in_dim(
+        jnp.zeros(shape, shard.dtype), shard, here * step_2, axis=1
+    )
+    going_up = going_down = shard
+    for far in range(1, ways // 2 + 1):
+        going_up = lax.ppermute(going_up, "tile", [(d, (d + 1) % ways) for d in range(ways)])
+        full = lax.dynamic_update_slice_in_dim(full, going_up, (here - far) % ways * step_2, axis=1)
+        if 2 * far < ways:
+            going_down = lax.ppermute(
+                going_down, "tile", [(d, (d - 1) % ways) for d in range(ways)]
+            )
+            full = lax.dynamic_update_slice_in_dim(
+                full, going_down, (here + far) % ways * step_2, axis=1
+            )
+    every = full
     column = lax.dynamic_slice_in_dim(coarse_inv, mine_index, 1, 1)
     mine = jnp.dot(every, column, precision=lax.Precision.HIGHEST)
     return schwarz + mine * coarse_vec

time: 374 us -> 421 us (1.13)
  starting transfers between devices: 41.9 us -> 101 us
  blocking collectives: 104 us -> 63.9 us
  waiting for transfers between devices: 2.86 us -> 28.1 us
    ppermute x0 -> x30, starting transfers between devices: none -> 63 us  [the longest x14 62.3 us: precondition(): lax.ppermute(going_down, 'tile', [(d, (d - 1) % ways) for d in range(ways)])]
    all_gather x2 -> x0, blocking collectives: 40.3 us -> none  [precondition(): every = lax.all_gather(restricted[:, None], 'tile', axis=1, tiled=True)]
    ppermute x0 -> x30, waiting for transfers between devices: none -> 25.3 us  [the longest x16 21.8 us: precondition(): lax.ppermute(going_up, 'tile', [(d, (d + 1) % ways) for d in range(ways)])]
  transfers between devices with their start and end apart: 16 -> 46, of which waited for: 4 -> 24; matrix products, arithmetic and copies ran while one was open for 48% -> 43% of each run, Pallas kernels for 0% -> 0%
where the time goes in v1:
time: 421 us; the launch traced here: 419 us
  other arithmetic  168 us (40%)
  starting transfers between devices  101 us (24%)
  blocking collectives  63.9 us (15%)
  matrix products  35.9 us (9%)
  waiting for transfers between devices  28.1 us (7%)
  local copies, waits for them, and re-layouts  21.2 us (5%)
    unnamed x4, other arithmetic  158 us
    psum x2, blocking collectives, both_dots(): return lax.psum((inner(resid, zvec), inner(image, zvec)), 'tile')  63.9 us
    ppermute x14, starting transfers between devices, precondition(): lax.ppermute(going_down, 'tile', [(d, (d - 1) % ways) for d in range(ways)])  62.3 us
    ppermute x8, starting transfers between devices, with_halo(): lax.ppermute(lax.slice_in_dim(block, block.shape[dim] - width, None, axis...  27.9 us
    dot_general x2, matrix products, operate(): contrib = jnp.dot(widened, stiffness, precision=lax.Precision.HIGHEST)  25.5 us
    ppermute x16, waiting for transfers between devices, precondition(): lax.ppermute(going_up, 'tile', [(d, (d + 1) % ways) for d in range(ways)])  21.8 us
    scatter-add x1, local copies, waits for them, and re-layouts, build_stiffness(): return jnp.zeros((SUB, SUB), jnp.float32).at[rows_idx, cols_idx].add(values)  18 us
    ppermute x8, starting transfers between devices, with_halo(): lax.ppermute(lax.slice_in_dim(block, 0, width, axis=dim), axis, backward)  10.3 us
  transfers between devices with their start and end apart: 46, of which 24 were waited for; matrix products, arithmetic and copies ran while one was open for 43% of the time, Pallas kernels for 0%

profile of v1, /device:TPU:0, one launch (start us, length us, event | category | flops | bytes accessed | tf_op | source)
XLA Modules:
  0.0 419.4 jit_solution(9729947994448643924)
XLA Ops:
  0.7 1.7 multiply_reduce_fusion.5
  2.9 5.0 %collective-permute-start.5 = (f32[128,1]{0,1:T(1,128)S(1)}, f32[128,1]{0,1:T(1,128)S(1)}, u32[]{:S(2)}, u32[]{:S(2)}) collective-permute-start(f32[128,1]{0,1:T(1,128)S(1)} %bitcast.22), channel_id=1, source_target_pairs={{0,15},{1,0},{2,1},{3,2},{4,3},{5,4},{6,5},{7,6},{8,7},{9,8},{10,9... | collective-permute-start | bytes 1544 | tf_op jit(solution)/shard_map/ppermute | solution.py:63
  7.9 1.3 collective-permute-start.1
  9.2 3.0 collective-permute-start
  12.2 1.1 compare_select_fusion.1
  13.8 1.1 multiply_reduce_fusion.6
  15.3 4.4 %collective-permute-start.7 = (f32[128,1]{0,1:T(1,128)S(1)}, f32[128,1]{0,1:T(1,128)S(1)}, u32[]{:S(2)}, u32[]{:S(2)}) collective-permute-start(f32[128,1]{0,1:T(1,128)S(1)} %collective-permute-done.5), channel_id=1, source_target_pairs={{0,15},{1,0},{2,1},{3,2},{4,3},{5,4},{6,5},{7,6},{8,7},{9,8},{10,9... | collective-permute-start | bytes 1544 | tf_op jit(solution)/shard_map/ppermute | solution.py:63
  19.7 1.2 collective-permute-done.6
  21.0 4.4 %collective-permute-start.9 = (f32[128,1]{0,1:T(1,128)S(1)}, f32[128,1]{0,1:T(1,128)S(1)}, u32[]{:S(2)}, u32[]{:S(2)}) collective-permute-start(f32[128,1]{0,1:T(1,128)S(1)} %collective-permute-done.7), channel_id=1, source_target_pairs={{0,15},{1,0},{2,1},{3,2},{4,3},{5,4},{6,5},{7,6},{8,7},{9,8},{10,9... | collective-permute-start | bytes 1544 | tf_op jit(solution)/shard_map/ppermute | solution.py:63
  25.4 1.2 collective-permute-done.8
  26.6 0.8 neg.4
  27.4 4.4 %collective-permute-start.11 = (f32[128,1]{0,1:T(1,128)S(1)}, f32[128,1]{0,1:T(1,128)S(1)}, u32[]{:S(2)}, u32[]{:S(2)}) collective-permute-start(f32[128,1]{0,1:T(1,128)S(1)} %collective-permute-done.9), channel_id=1, source_target_pairs={{0,15},{1,0},{2,1},{3,2},{4,3},{5,4},{6,5},{7,6},{8,7},{9,8},{10,9... | collective-permute-start | bytes 1544 | tf_op jit(solution)/shard_map/ppermute | solution.py:63
  32.4 0.7 collective-permute-done.11
  33.1 4.4 %collective-permute-start.13 = (f32[128,1]{0,1:T(1,128)S(1)}, f32[128,1]{0,1:T(1,128)S(1)}, u32[]{:S(2)}, u32[]{:S(2)}) collective-permute-start(f32[128,1]{0,1:T(1,128)S(1)} %collective-permute-done.11), channel_id=1, source_target_pairs={{0,15},{1,0},{2,1},{3,2},{4,3},{5,4},{6,5},{7,6},{8,7},{9,8},{10,9... | collective-permute-start | bytes 1544 | tf_op jit(solution)/shard_map/ppermute | solution.py:63
  38.0 0.8 collective-permute-done.13
  38.8 4.4 %collective-permute-start.15 = (f32[128,1]{0,1:T(1,128)S(1)}, f32[128,1]{0,1:T(1,128)S(1)}, u32[]{:S(2)}, u32[]{:S(2)}) collective-permute-start(f32[128,1]{0,1:T(1,128)S(1)} %collective-permute-done.13), channel_id=1, source_target_pairs={{0,15},{1,0},{2,1},{3,2},{4,3},{5,4},{6,5},{7,6},{8,7},{9,8},{10,9... | collective-permute-start | bytes 1544 | tf_op jit(solution)/shard_map/ppermute | solution.py:63
  44.5 4.4 %collective-permute-start.17 = (f32[128,1]{0,1:T(1,128)S(1)}, f32[128,1]{0,1:T(1,128)S(1)}, u32[]{:S(2)}, u32[]{:S(2)}) collective-permute-start(f32[128,1]{0,1:T(1,128)S(1)} %collective-permute-done.15), channel_id=1, source_target_pairs={{0,15},{1,0},{2,1},{3,2},{4,3},{5,4},{6,5},{7,6},{8,7},{9,8},{10,9... | collective-permute-start | bytes 1544 | tf_op jit(solution)/shard_map/ppermute | solution.py:63
  50.2 4.9 %collective-permute-done.18 = f32[128,1]{0,1:T(1,128)S(1)} collective-permute-done((f32[128,1]{0,1:T(1,128)S(1)}, f32[128,1]{0,1:T(1,128)S(1)}, u32[]{:S(2)}, u32[]{:S(2)}) %collective-permute-start.18) | collective-permute-done | bytes 544 | tf_op jit(solution)/shard_map/ppermute | solution.py:60
  55.1 4.7 %fusion.40 = (bf16[128,2048]{1,0:T(8,128)(2,1)S(1)}, f32[128,2048]{1,0:T(8,128)S(1)}) fusion(bf16[2048,2048]{1,0:T(8,128)(2,1)} %param.13, bf16[128,128]{1,0:T(8,128)(2,1)S(1)} %collective-permute-done.1, bf16[128,1792]{1,0:T(8,128)(2,1)S(1)} %get-tuple-element.29, bf16[128,128]{1,0:T(8,128)(2,1)S(1)} %collective-permute-done), kind=kOutput, calls=%fused_computation.86 | convolution fusion | flops 1075576832 | bytes 10485760 | tf_op jit(solution)/shard_map/dot_general | solution.py:48
  59.9 1.3 collective-permute-start.3
  61.2 3.0 collective-permute-start.2
  64.4 0.6 collective-permute-done.2
  65.2 1.3 collective-permute-start.20
  66.5 3.0 collective-permute-start.19
  69.6 156.5 %scatter_custom_fusion = f32[4194304]{0:T(1024)} fusion(s32[28672]{0:T(1024)S(1)} %broadcast_select_fusion, f32[28672]{0:T(1024)S(1)} %pad_maximum_fusion, f32[]{:T(128)} %constant.121.clone.1), kind=kCustom, calls=%fused_computation.1 | custom fusion | flops 28672 | bytes 16777220
  226.1 18.0 %reshape.335 = f32[2048,2048]{1,0:T(8,128)} reshape(f32[4194304]{0:T(1024)} %scatter_custom_fusion) | data formatting | bytes 33554432 | tf_op jit(solution)/shard_map/scatter-add | solution.py:37
  244.1 12.8 %fusion.41 = (bf16[128,2048]{1,0:T(8,128)(2,1)S(1)}, f32[128,2048]{1,0:T(8,128)S(1)}) fusion(f32[2048,2048]{1,0:T(8,128)} %reshape.335, f32[128,128]{1,0:T(8,128)S(1)} %collective-permute-done.20, f32[128,1792]{1,0:T(8,128)S(1)} %maximum_add_fusion, f32[128,128]{1,0:T(8,128)S(1)} %collective-permute-done.19), kind=kOutput, calls=%fused_computation.87 | convolution fusion | flops 6443237376 | bytes 19398656 | tf_op jit(solution)/shard_map/dot_general | solution.py:42
  257.0 1.3 collective-permute-start.22
  258.3 4.5 %collective-permute-start.21 = (bf16[128,128]{1,0:T(8,128)(2,1)S(1)}, bf16[128,128]{1,0:T(8,128)(2,1)S(1)}, u32[]{:S(2)}, u32[]{:S(2)}) collective-permute-start(bf16[128,128]{1,0:T(8,128)(2,1)S(1)} %get-tuple-element.34), channel_id=1, source_target_pairs={{0,1},{1,2},{2,3},{3,4},{4,5},{5,6},{6,7},{7,8},{8,9},{9,10},{10,1... | collective-permute-start | bytes 98312 | tf_op jit(solution)/shard_map/ppermute | solution.py:16
  262.9 0.8 collective-permute-done.21
  264.0 31.4 %all-reduce.1 = (f32[128]{0:T(128)S(1)}, f32[128]{0:T(128)S(1)}) all-reduce(f32[128]{0:T(128)S(1)} %get-tuple-element.5, f32[128]{0:T(128)S(1)} %get-tuple-element.4), channel_id=1, replica_groups=mesh['grp'=2,'tile'=16] {'tile'}, use_global_device_ids=true, to_apply=%region_2.3 | all-reduce | flops 256 | bytes 2048 | tf_op jit(solution)/shard_map/psum | solution.py:80
  296.0 1.2 multiply_reduce_fusion.2
  297.3 1.3 collective-permute-start.24
  298.6 3.0 collective-permute-start.23
  301.7 4.4 %collective-permute-start.28 = (f32[128,1]{0,1:T(1,128)S(1)}, f32[128,1]{0,1:T(1,128)S(1)}, u32[]{:S(2)}, u32[]{:S(2)}) collective-permute-start(f32[128,1]{0,1:T(1,128)S(1)} %bitcast.25), channel_id=1, source_target_pairs={{0,15},{1,0},{2,1},{3,2},{4,3},{5,4},{6,5},{7,6},{8,7},{9,8},{10,9... | collective-permute-start | bytes 1544 | tf_op jit(solution)/shard_map/ppermute | solution.py:63
  306.1 1.2 collective-permute-done.27
  307.4 4.4 %collective-permute-start.30 = (f32[128,1]{0,1:T(1,128)S(1)}, f32[128,1]{0,1:T(1,128)S(1)}, u32[]{:S(2)}, u32[]{:S(2)}) collective-permute-start(f32[128,1]{0,1:T(1,128)S(1)} %collective-permute-done.28), channel_id=1, source_target_pairs={{0,15},{1,0},{2,1},{3,2},{4,3},{5,4},{6,5},{7,6},{8,7},{9,8},{10,9... | collective-permute-start | bytes 1544 | tf_op jit(solution)/shard_map/ppermute | solution.py:63
  311.8 1.2 collective-permute-done.29
  313.1 4.4 %collective-permute-start.32 = (f32[128,1]{0,1:T(1,128)S(1)}, f32[128,1]{0,1:T(1,128)S(1)}, u32[]{:S(2)}, u32[]{:S(2)}) collective-permute-start(f32[128,1]{0,1:T(1,128)S(1)} %collective-permute-done.30), channel_id=1, source_target_pairs={{0,15},{1,0},{2,1},{3,2},{4,3},{5,4},{6,5},{7,6},{8,7},{9,8},{10,9... | collective-permute-start | bytes 1544 | tf_op jit(solution)/shard_map/ppermute | solution.py:63
  317.5 1.2 collective-permute-done.31
  318.8 4.4 %collective-permute-start.34 = (f32[128,1]{0,1:T(1,128)S(1)}, f32[128,1]{0,1:T(1,128)S(1)}, u32[]{:S(2)}, u32[]{:S(2)}) collective-permute-start(f32[128,1]{0,1:T(1,128)S(1)} %collective-permute-done.32), channel_id=1, source_target_pairs={{0,15},{1,0},{2,1},{3,2},{4,3},{5,4},{6,5},{7,6},{8,7},{9,8},{10,9... | collective-permute-start | bytes 1544 | tf_op jit(solution)/shard_map/ppermute | solution.py:63
  323.2 1.2 collective-permute-done.33
  324.5 4.4 %collective-permute-start.36 = (f32[128,1]{0,1:T(1,128)S(1)}, f32[128,1]{0,1:T(1,128)S(1)}, u32[]{:S(2)}, u32[]{:S(2)}) collective-permute-start(f32[128,1]{0,1:T(1,128)S(1)} %collective-permute-done.34), channel_id=1, source_target_pairs={{0,15},{1,0},{2,1},{3,2},{4,3},{5,4},{6,5},{7,6},{8,7},{9,8},{10,9... | collective-permute-start | bytes 1544 | tf_op jit(solution)/shard_map/ppermute | solution.py:63
  328.9 1.2 collective-permute-done.35
  330.2 4.4 %collective-permute-start.38 = (f32[128,1]{0,1:T(1,128)S(1)}, f32[128,1]{0,1:T(1,128)S(1)}, u32[]{:S(2)}, u32[]{:S(2)}) collective-permute-start(f32[128,1]{0,1:T(1,128)S(1)} %collective-permute-done.36), channel_id=1, source_target_pairs={{0,15},{1,0},{2,1},{3,2},{4,3},{5,4},{6,5},{7,6},{8,7},{9,8},{10,9... | collective-permute-start | bytes 1544 | tf_op jit(solution)/shard_map/ppermute | solution.py:63
  334.6 1.2 collective-permute-done.37
  335.8 0.7 dynamic_update_slice.112
  336.7 4.5 %collective-permute-start.40 = (f32[128,1]{0,1:T(1,128)S(1)}, f32[128,1]{0,1:T(1,128)S(1)}, u32[]{:S(2)}, u32[]{:S(2)}) collective-permute-start(f32[128,1]{0,1:T(1,128)S(1)} %collective-permute-done.38), channel_id=1, source_target_pairs={{0,15},{1,0},{2,1},{3,2},{4,3},{5,4},{6,5},{7,6},{8,7},{9,8},{10,9... | collective-permute-start | bytes 1544 | tf_op jit(solution)/shard_map/ppermute | solution.py:63
  341.8 0.7 collective-permute-done.40
  342.5 4.7 %collective-permute-done.41 = f32[128,1]{0,1:T(1,128)S(1)} collective-permute-done((f32[128,1]{0,1:T(1,128)S(1)}, f32[128,1]{0,1:T(1,128)S(1)}, u32[]{:S(2)}, u32[]{:S(2)}) %collective-permute-start.41) | collective-permute-done | bytes 544 | tf_op jit(solution)/shard_map/ppermute | solution.py:60
  347.2 4.7 %fusion.42 = (bf16[128,2048]{1,0:T(8,128)(2,1)S(1)}, f32[128,2048]{1,0:T(8,128)S(1)}) fusion(bf16[2048,2048]{1,0:T(8,128)(2,1)} %param.13, bf16[128,128]{1,0:T(8,128)(2,1)S(1)} %collective-permute-done.24, bf16[128,1792]{1,0:T(8,128)(2,1)S(1)} %convert_element_type.25, bf16[128,128]{1,0:T(8,128)(2,1)S(1)} %collective-permute-done.23), kind=kOutput, calls=%fused_computation.88 | convolution fusion | flops 1075576832 | bytes 10485760 | tf_op jit(solution)/shard_map/dot_general | solution.py:48
  352.0 1.3 collective-permute-start.26
  353.3 3.0 collective-permute-start.25
  356.3 0.8 convolution_bitcast_fusion
  357.4 1.3 collective-permute-start.43
  358.7 3.3 collective-permute-start.42
  362.0 0.7 collective-permute-done.42
  362.6 12.7 %fusion.43 = (bf16[128,2048]{1,0:T(8,128)(2,1)S(1)}, f32[128,2048]{1,0:T(8,128)S(1)}) fusion(f32[2048,2048]{1,0:T(8,128)} %reshape.335, f32[128,128]{1,0:T(8,128)S(1)} %collective-permute-done.43, f32[128,1792]{1,0:T(8,128)S(1)} %maximum_add_fusion.2, f32[128,128]{1,0:T(8,128)S(1)} %collective-permute-done.42), kind=kOutput, calls=%fused_computation.89 | convolution fusion | flops 6443237376 | bytes 19398656 | tf_op jit(solution)/shard_map/dot_general | solution.py:42
  375.4 1.3 collective-permute-start.45
  376.7 4.9 %collective-permute-start.44 = (bf16[128,128]{1,0:T(8,128)(2,1)S(1)}, bf16[128,128]{1,0:T(8,128)(2,1)S(1)}, u32[]{:S(2)}, u32[]{:S(2)}) collective-permute-start(bf16[128,128]{1,0:T(8,128)(2,1)S(1)} %get-tuple-element.30), channel_id=1, source_target_pairs={{0,1},{1,2},{2,3},{3,4},{4,5},{5,6},{6,7},{7,8},{8,9},{9,10},{10,1... | collective-permute-start | bytes 98312 | tf_op jit(solution)/shard_map/ppermute | solution.py:16
  381.7 0.8 collective-permute-done.44
  383.1 32.5 %all-reduce = (f32[128]{0:T(128)}, f32[128]{0:T(128)}) all-reduce(f32[128]{0:T(128)S(1)} %get-tuple-element.3, f32[128]{0:T(128)S(1)} %get-tuple-element.2), channel_id=1, replica_groups=mesh['grp'=2,'tile'=16] {'tile'}, use_global_device_ids=true, to_apply=%region_8.9 | all-reduce | flops 256 | bytes 2048 | tf_op jit(solution)/shard_map/psum | solution.py:80
  415.6 0.7 subtract_divide_fusion
  416.3 3.1 multiply_subtract_fusion
  (137 shorter events, 8.4 us)
Async XLA Ops:
  0.6 43.1 %copy-start = (f32[16,16]{1,0:T(8,128)S(1)}, f32[16,16]{1,0:T(8,128)}, u32[]{:S(2)}) copy-start(f32[16,16]{1,0:T(8,128)} %param.15) | copy-start | bytes 3076
  0.6 64.4 %copy-start.7 = (f32[1792]{0:T(1024)S(1)}, f32[1792]{0:T(1024)}, u32[]{:S(2)}) copy-start(f32[1792]{0:T(1024)} %param.14) | copy-start | bytes 21508
  0.7 68.9 %copy-start.10 = (f32[7168]{0:T(1024)S(1)}, f32[7168]{0:T(1024)}, u32[]{:S(2)}) copy-start(f32[7168]{0:T(1024)} %param.12) | copy-start | bytes 86020
  2.3 12.8 %collective-permute-start.4 = (f32[128,1]{0,1:T(1,128)S(1)}, f32[128,1]{0,1:T(1,128)S(1)}, u32[]{:S(2)}, u32[]{:S(2)}) collective-permute-start(f32[128,1]{0,1:T(1,128)S(1)} %bitcast.21), channel_id=1, source_target_pairs={{0,1},{1,2},{2,3},{3,4},{4,5},{5,6},{6,7},{7,8},{8,9},{9,10},{10,1... | collective-permute-start | bytes 1544 | tf_op jit(solution)/shard_map/ppermute | solution.py:60
  2.9 12.4 %collective-permute-start.5 = (f32[128,1]{0,1:T(1,128)S(1)}, f32[128,1]{0,1:T(1,128)S(1)}, u32[]{:S(2)}, u32[]{:S(2)}) collective-permute-start(f32[128,1]{0,1:T(1,128)S(1)} %bitcast.22), channel_id=1, source_target_pairs={{0,15},{1,0},{2,1},{3,2},{4,3},{5,4},{6,5},{7,6},{8,7},{9,8},{10,9... | collective-permute-start | bytes 1544 | tf_op jit(solution)/shard_map/ppermute | solution.py:63
  7.9 47.2 %collective-permute-start.1 = (bf16[128,128]{1,0:T(8,128)(2,1)S(1)}, bf16[128,128]{1,0:T(8,128)(2,1)S(1)}, u32[]{:S(2)}, u32[]{:S(2)}) collective-permute-start(bf16[128,128]{1,0:T(8,128)(2,1)S(1)} %get-tuple-element.41), channel_id=1, source_target_pairs={{1,0},{2,1},{3,2},{4,3},{5,4},{6,5},{7,6},{8,7},{9,8},{10,9},{11,1... | collective-permute-start | bytes 98312 | tf_op jit(solution)/shard_map/ppermute | solution.py:19
  9.2 45.9 %collective-permute-start = (bf16[128,128]{1,0:T(8,128)(2,1)S(1)}, bf16[128,128]{1,0:T(8,128)(2,1)S(1)}, u32[]{:S(2)}, u32[]{:S(2)}) collective-permute-start(bf16[128,128]{1,0:T(8,128)(2,1)S(1)} %get-tuple-element.40), channel_id=1, source_target_pairs={{0,1},{1,2},{2,3},{3,4},{4,5},{5,6},{6,7},{7,8},{8,9},{9,10},{10,1... | collective-permute-start | bytes 98312 | tf_op jit(solution)/shard_map/ppermute | solution.py:16
  15.2 5.7 %collective-permute-start.6 = (f32[128,1]{0,1:T(1,128)S(1)}, f32[128,1]{0,1:T(1,128)S(1)}, u32[]{:S(2)}, u32[]{:S(2)}) collective-permute-start(f32[128,1]{0,1:T(1,128)S(1)} %collective-permute-done.4), channel_id=1, source_target_pairs={{0,1},{1,2},{2,3},{3,4},{4,5},{5,6},{6,7},{7,8},{8,9},{9,10},{10,1... | collective-permute-start | bytes 1544 | tf_op jit(solution)/shard_map/ppermute | solution.py:60
  15.3 5.7 %collective-permute-start.7 = (f32[128,1]{0,1:T(1,128)S(1)}, f32[128,1]{0,1:T(1,128)S(1)}, u32[]{:S(2)}, u32[]{:S(2)}) collective-permute-start(f32[128,1]{0,1:T(1,128)S(1)} %collective-permute-done.5), channel_id=1, source_target_pairs={{0,15},{1,0},{2,1},{3,2},{4,3},{5,4},{6,5},{7,6},{8,7},{9,8},{10,9... | collective-permute-start | bytes 1544 | tf_op jit(solution)/shard_map/ppermute | solution.py:63
  20.9 5.7 %collective-permute-start.8 = (f32[128,1]{0,1:T(1,128)S(1)}, f32[128,1]{0,1:T(1,128)S(1)}, u32[]{:S(2)}, u32[]{:S(2)}) collective-permute-start(f32[128,1]{0,1:T(1,128)S(1)} %collective-permute-done.6), channel_id=1, source_target_pairs={{0,1},{1,2},{2,3},{3,4},{4,5},{5,6},{6,7},{7,8},{8,9},{9,10},{10,1... | collective-permute-start | bytes 1544 | tf_op jit(solution)/shard_map/ppermute | solution.py:60
  21.0 6.4 %collective-permute-start.9 = (f32[128,1]{0,1:T(1,128)S(1)}, f32[128,1]{0,1:T(1,128)S(1)}, u32[]{:S(2)}, u32[]{:S(2)}) collective-permute-start(f32[128,1]{0,1:T(1,128)S(1)} %collective-permute-done.7), channel_id=1, source_target_pairs={{0,15},{1,0},{2,1},{3,2},{4,3},{5,4},{6,5},{7,6},{8,7},{9,8},{10,9... | collective-permute-start | bytes 1544 | tf_op jit(solution)/shard_map/ppermute | solution.py:63
  26.6 5.7 %collective-permute-start.10 = (f32[128,1]{0,1:T(1,128)S(1)}, f32[128,1]{0,1:T(1,128)S(1)}, u32[]{:S(2)}, u32[]{:S(2)}) collective-permute-start(f32[128,1]{0,1:T(1,128)S(1)} %collective-permute-done.8), channel_id=1, source_target_pairs={{0,1},{1,2},{2,3},{3,4},{4,5},{5,6},{6,7},{7,8},{8,9},{9,10},{10,1... | collective-permute-start | bytes 1544 | tf_op jit(solution)/shard_map/ppermute | solution.py:60
  27.4 5.7 %collective-permute-start.11 = (f32[128,1]{0,1:T(1,128)S(1)}, f32[128,1]{0,1:T(1,128)S(1)}, u32[]{:S(2)}, u32[]{:S(2)}) collective-permute-start(f32[128,1]{0,1:T(1,128)S(1)} %collective-permute-done.9), channel_id=1, source_target_pairs={{0,15},{1,0},{2,1},{3,2},{4,3},{5,4},{6,5},{7,6},{8,7},{9,8},{10,9... | collective-permute-start | bytes 1544 | tf_op jit(solution)/shard_map/ppermute | solution.py:63
  32.3 5.7 %collective-permute-start.12 = (f32[128,1]{0,1:T(1,128)S(1)}, f32[128,1]{0,1:T(1,128)S(1)}, u32[]{:S(2)}, u32[]{:S(2)}) collective-permute-start(f32[128,1]{0,1:T(1,128)S(1)} %collective-permute-done.10), channel_id=1, source_target_pairs={{0,1},{1,2},{2,3},{3,4},{4,5},{5,6},{6,7},{7,8},{8,9},{9,10},{10,1... | collective-permute-start | bytes 1544 | tf_op jit(solution)/shard_map/ppermute | solution.py:60
  33.1 5.7 %collective-permute-start.13 = (f32[128,1]{0,1:T(1,128)S(1)}, f32[128,1]{0,1:T(1,128)S(1)}, u32[]{:S(2)}, u32[]{:S(2)}) collective-permute-start(f32[128,1]{0,1:T(1,128)S(1)} %collective-permute-done.11), channel_id=1, source_target_pairs={{0,15},{1,0},{2,1},{3,2},{4,3},{5,4},{6,5},{7,6},{8,7},{9,8},{10,9... | collective-permute-start | bytes 1544 | tf_op jit(solution)/shard_map/ppermute | solution.py:63
  38.0 5.7 %collective-permute-start.14 = (f32[128,1]{0,1:T(1,128)S(1)}, f32[128,1]{0,1:T(1,128)S(1)}, u32[]{:S(2)}, u32[]{:S(2)}) collective-permute-start(f32[128,1]{0,1:T(1,128)S(1)} %collective-permute-done.12), channel_id=1, source_target_pairs={{0,1},{1,2},{2,3},{3,4},{4,5},{5,6},{6,7},{7,8},{8,9},{9,10},{10,1... | collective-permute-start | bytes 1544 | tf_op jit(solution)/shard_map/ppermute | solution.py:60
  38.8 5.7 %collective-permute-start.15 = (f32[128,1]{0,1:T(1,128)S(1)}, f32[128,1]{0,1:T(1,128)S(1)}, u32[]{:S(2)}, u32[]{:S(2)}) collective-permute-start(f32[128,1]{0,1:T(1,128)S(1)} %collective-permute-done.13), channel_id=1, source_target_pairs={{0,15},{1,0},{2,1},{3,2},{4,3},{5,4},{6,5},{7,6},{8,7},{9,8},{10,9... | collective-permute-start | bytes 1544 | tf_op jit(solution)/shard_map/ppermute | solution.py:63
  43.7 5.7 %collective-permute-start.16 = (f32[128,1]{0,1:T(1,128)S(1)}, f32[128,1]{0,1:T(1,128)S(1)}, u32[]{:S(2)}, u32[]{:S(2)}) collective-permute-start(f32[128,1]{0,1:T(1,128)S(1)} %collective-permute-done.14), channel_id=1, source_target_pairs={{0,1},{1,2},{2,3},{3,4},{4,5},{5,6},{6,7},{7,8},{8,9},{9,10},{10,1... | collective-permute-start | bytes 1544 | tf_op jit(solution)/shard_map/ppermute | solution.py:60
  43.9 22.7 %copy-start.11 = (f32[16]{0:T(128)}, f32[16]{0:T(128)S(1)}, u32[]{:S(2)}) copy-start(f32[16]{0:T(128)S(1)} %dynamic-slice_reduce_fusion) | copy-start | bytes 196
  44.5 5.7 %collective-permute-start.17 = (f32[128,1]{0,1:T(1,128)S(1)}, f32[128,1]{0,1:T(1,128)S(1)}, u32[]{:S(2)}, u32[]{:S(2)}) collective-permute-start(f32[128,1]{0,1:T(1,128)S(1)} %collective-permute-done.15), channel_id=1, source_target_pairs={{0,15},{1,0},{2,1},{3,2},{4,3},{5,4},{6,5},{7,6},{8,7},{9,8},{10,9... | collective-permute-start | bytes 1544 | tf_op jit(solution)/shard_map/ppermute | solution.py:63
  49.4 5.7 %collective-permute-start.18 = (f32[128,1]{0,1:T(1,128)S(1)}, f32[128,1]{0,1:T(1,128)S(1)}, u32[]{:S(2)}, u32[]{:S(2)}) collective-permute-start(f32[128,1]{0,1:T(1,128)S(1)} %collective-permute-done.16), channel_id=1, source_target_pairs={{0,1},{1,2},{2,3},{3,4},{4,5},{5,6},{6,7},{7,8},{8,9},{9,10},{10,1... | collective-permute-start | bytes 1544 | tf_op jit(solution)/shard_map/ppermute | solution.py:60
  59.9 4.5 %collective-permute-start.3 = (bf16[128,128]{1,0:T(8,128)(2,1)S(1)}, bf16[128,128]{1,0:T(8,128)(2,1)S(1)}, u32[]{:S(2)}, u32[]{:S(2)}) collective-permute-start(bf16[128,128]{1,0:T(8,128)(2,1)S(1)} %get-tuple-element.37), channel_id=1, source_target_pairs={{1,0},{2,1},{3,2},{4,3},{5,4},{6,5},{7,6},{8,7},{9,8},{10,9},{11,1... | collective-permute-start | bytes 98312 | tf_op jit(solution)/shard_map/ppermute | solution.py:19
  61.2 3.9 collective-permute-start.2
  65.2 178.9 %collective-permute-start.20 = (f32[128,128]{1,0:T(8,128)S(1)}, f32[128,128]{1,0:T(8,128)S(1)}, u32[]{:S(2)}, u32[]{:S(2)}) collective-permute-start(f32[128,128]{1,0:T(8,128)S(1)} %get-tuple-element.27), channel_id=1, source_target_pairs={{1,0},{2,1},{3,2},{4,3},{5,4},{6,5},{7,6},{8,7},{9,8},{10,9},{11,1... | collective-permute-start | bytes 196616 | tf_op jit(solution)/shard_map/ppermute | solution.py:19
  66.5 177.6 %collective-permute-start.19 = (f32[128,128]{1,0:T(8,128)S(1)}, f32[128,128]{1,0:T(8,128)S(1)}, u32[]{:S(2)}, u32[]{:S(2)}) collective-permute-start(f32[128,128]{1,0:T(8,128)S(1)} %get-tuple-element.26), channel_id=1, source_target_pairs={{0,1},{1,2},{2,3},{3,4},{4,5},{5,6},{6,7},{7,8},{8,9},{9,10},{10,1... | collective-permute-start | bytes 196616 | tf_op jit(solution)/shard_map/ppermute | solution.py:16
  244.1 19.6 %copy-start.1 = (f32[128,1792]{1,0:T(8,128)S(1)}, f32[128,1792]{1,0:T(8,128)}, u32[]{:S(2)}) copy-start(f32[128,1792]{1,0:T(8,128)} %param.8) | copy-start | bytes 2752516
  244.1 19.6 %copy-start.8 = (f32[1792]{0:T(1024)S(1)}, f32[1792]{0:T(1024)}, u32[]{:S(2)}) copy-start(f32[1792]{0:T(1024)} %param.9) | copy-start | bytes 21508
  257.0 5.9 %collective-permute-start.22 = (bf16[128,128]{1,0:T(8,128)(2,1)S(1)}, bf16[128,128]{1,0:T(8,128)(2,1)S(1)}, u32[]{:S(2)}, u32[]{:S(2)}) collective-permute-start(bf16[128,128]{1,0:T(8,128)(2,1)S(1)} %get-tuple-element.35), channel_id=1, source_target_pairs={{1,0},{2,1},{3,2},{4,3},{5,4},{6,5},{7,6},{8,7},{9,8},{10,9},{11,1... | collective-permute-start | bytes 98312 | tf_op jit(solution)/shard_map/ppermute | solution.py:19
  258.3 5.4 %collective-permute-start.21 = (bf16[128,128]{1,0:T(8,128)(2,1)S(1)}, bf16[128,128]{1,0:T(8,128)(2,1)S(1)}, u32[]{:S(2)}, u32[]{:S(2)}) collective-permute-start(bf16[128,128]{1,0:T(8,128)(2,1)S(1)} %get-tuple-element.34), channel_id=1, source_target_pairs={{0,1},{1,2},{2,3},{3,4},{4,5},{5,6},{6,7},{7,8},{8,9},{9,10},{10,1... | collective-permute-start | bytes 98312 | tf_op jit(solution)/shard_map/ppermute | solution.py:16
  263.7 31.7 %copy-start.3 = (f32[128,128]{1,0:T(8,128)}, f32[128,128]{1,0:T(8,128)S(1)}, u32[]{:S(2)}) copy-start(f32[128,128]{1,0:T(8,128)S(1)} %get-tuple-element.20) | copy-start | bytes 196612
  263.7 31.7 %copy-start.4 = (f32[128,128]{1,0:T(8,128)}, f32[128,128]{1,0:T(8,128)S(1)}, u32[]{:S(2)}) copy-start(f32[128,128]{1,0:T(8,128)S(1)} %get-tuple-element.21) | copy-start | bytes 196612
  295.4 0.6 copy-start.14
  295.4 0.6 copy-start.15
  296.0 39.8 %copy-start.12 = (f32[128]{0:T(128)}, f32[128]{0:T(128)S(1)}, u32[]{:S(2)}) copy-start(f32[128]{0:T(128)S(1)} %div.12) | copy-start | bytes 1540
  297.2 38.6 %copy-start.13 = (f32[128]{0:T(128)}, f32[128]{0:T(128)S(1)}, u32[]{:S(2)}) copy-start(f32[128]{0:T(128)S(1)} %get-tuple-element.12) | copy-start | bytes 1540
  297.3 50.0 %collective-permute-start.24 = (bf16[128,128]{1,0:T(8,128)(2,1)S(1)}, bf16[128,128]{1,0:T(8,128)(2,1)S(1)}, u32[]{:S(2)}, u32[]{:S(2)}) collective-permute-start(bf16[128,128]{1,0:T(8,128)(2,1)S(1)} %get-tuple-element.39), channel_id=1, source_target_pairs={{1,0},{2,1},{3,2},{4,3},{5,4},{6,5},{7,6},{8,7},{9,8},{10,9},{11,1... | collective-permute-start | bytes 98312 | tf_op jit(solution)/shard_map/ppermute | solution.py:19
  298.6 48.7 %collective-permute-start.23 = (bf16[128,128]{1,0:T(8,128)(2,1)S(1)}, bf16[128,128]{1,0:T(8,128)(2,1)S(1)}, u32[]{:S(2)}, u32[]{:S(2)}) collective-permute-start(bf16[128,128]{1,0:T(8,128)(2,1)S(1)} %get-tuple-element.38), channel_id=1, source_target_pairs={{0,1},{1,2},{2,3},{3,4},{4,5},{5,6},{6,7},{7,8},{8,9},{9,10},{10,1... | collective-permute-start | bytes 98312 | tf_op jit(solution)/shard_map/ppermute | solution.py:16
  301.6 5.7 %collective-permute-start.27 = (f32[128,1]{0,1:T(1,128)S(1)}, f32[128,1]{0,1:T(1,128)S(1)}, u32[]{:S(2)}, u32[]{:S(2)}) collective-permute-start(f32[128,1]{0,1:T(1,128)S(1)} %bitcast.24), channel_id=1, source_target_pairs={{0,1},{1,2},{2,3},{3,4},{4,5},{5,6},{6,7},{7,8},{8,9},{9,10},{10,1... | collective-permute-start | bytes 1544 | tf_op jit(solution)/shard_map/ppermute | solution.py:60
  301.7 5.7 %collective-permute-start.28 = (f32[128,1]{0,1:T(1,128)S(1)}, f32[128,1]{0,1:T(1,128)S(1)}, u32[]{:S(2)}, u32[]{:S(2)}) collective-permute-start(f32[128,1]{0,1:T(1,128)S(1)} %bitcast.25), channel_id=1, source_target_pairs={{0,15},{1,0},{2,1},{3,2},{4,3},{5,4},{6,5},{7,6},{8,7},{9,8},{10,9... | collective-permute-start | bytes 1544 | tf_op jit(solution)/shard_map/ppermute | solution.py:63
  307.3 5.7 %collective-permute-start.29 = (f32[128,1]{0,1:T(1,128)S(1)}, f32[128,1]{0,1:T(1,128)S(1)}, u32[]{:S(2)}, u32[]{:S(2)}) collective-permute-start(f32[128,1]{0,1:T(1,128)S(1)} %collective-permute-done.27), channel_id=1, source_target_pairs={{0,1},{1,2},{2,3},{3,4},{4,5},{5,6},{6,7},{7,8},{8,9},{9,10},{10,1... | collective-permute-start | bytes 1544 | tf_op jit(solution)/shard_map/ppermute | solution.py:60
  307.4 5.7 %collective-permute-start.30 = (f32[128,1]{0,1:T(1,128)S(1)}, f32[128,1]{0,1:T(1,128)S(1)}, u32[]{:S(2)}, u32[]{:S(2)}) collective-permute-start(f32[128,1]{0,1:T(1,128)S(1)} %collective-permute-done.28), channel_id=1, source_target_pairs={{0,15},{1,0},{2,1},{3,2},{4,3},{5,4},{6,5},{7,6},{8,7},{9,8},{10,9... | collective-permute-start | bytes 1544 | tf_op jit(solution)/shard_map/ppermute | solution.py:63
  313.0 5.7 %collective-permute-start.31 = (f32[128,1]{0,1:T(1,128)S(1)}, f32[128,1]{0,1:T(1,128)S(1)}, u32[]{:S(2)}, u32[]{:S(2)}) collective-permute-start(f32[128,1]{0,1:T(1,128)S(1)} %collective-permute-done.29), channel_id=1, source_target_pairs={{0,1},{1,2},{2,3},{3,4},{4,5},{5,6},{6,7},{7,8},{8,9},{9,10},{10,1... | collective-permute-start | bytes 1544 | tf_op jit(solution)/shard_map/ppermute | solution.py:60
  313.1 5.7 %collective-permute-start.32 = (f32[128,1]{0,1:T(1,128)S(1)}, f32[128,1]{0,1:T(1,128)S(1)}, u32[]{:S(2)}, u32[]{:S(2)}) collective-permute-start(f32[128,1]{0,1:T(1,128)S(1)} %collective-permute-done.30), channel_id=1, source_target_pairs={{0,15},{1,0},{2,1},{3,2},{4,3},{5,4},{6,5},{7,6},{8,7},{9,8},{10,9... | collective-permute-start | bytes 1544 | tf_op jit(solution)/shard_map/ppermute | solution.py:63
  318.7 5.7 %collective-permute-start.33 = (f32[128,1]{0,1:T(1,128)S(1)}, f32[128,1]{0,1:T(1,128)S(1)}, u32[]{:S(2)}, u32[]{:S(2)}) collective-permute-start(f32[128,1]{0,1:T(1,128)S(1)} %collective-permute-done.31), channel_id=1, source_target_pairs={{0,1},{1,2},{2,3},{3,4},{4,5},{5,6},{6,7},{7,8},{8,9},{9,10},{10,1... | collective-permute-start | bytes 1544 | tf_op jit(solution)/shard_map/ppermute | solution.py:60
  318.8 5.7 %collective-permute-start.34 = (f32[128,1]{0,1:T(1,128)S(1)}, f32[128,1]{0,1:T(1,128)S(1)}, u32[]{:S(2)}, u32[]{:S(2)}) collective-permute-start(f32[128,1]{0,1:T(1,128)S(1)} %collective-permute-done.32), channel_id=1, source_target_pairs={{0,15},{1,0},{2,1},{3,2},{4,3},{5,4},{6,5},{7,6},{8,7},{9,8},{10,9... | collective-permute-start | bytes 1544 | tf_op jit(solution)/shard_map/ppermute | solution.py:63
  324.4 5.7 %collective-permute-start.35 = (f32[128,1]{0,1:T(1,128)S(1)}, f32[128,1]{0,1:T(1,128)S(1)}, u32[]{:S(2)}, u32[]{:S(2)}) collective-permute-start(f32[128,1]{0,1:T(1,128)S(1)} %collective-permute-done.33), channel_id=1, source_target_pairs={{0,1},{1,2},{2,3},{3,4},{4,5},{5,6},{6,7},{7,8},{8,9},{9,10},{10,1... | collective-permute-start | bytes 1544 | tf_op jit(solution)/shard_map/ppermute | solution.py:60
  324.5 5.7 %collective-permute-start.36 = (f32[128,1]{0,1:T(1,128)S(1)}, f32[128,1]{0,1:T(1,128)S(1)}, u32[]{:S(2)}, u32[]{:S(2)}) collective-permute-start(f32[128,1]{0,1:T(1,128)S(1)} %collective-permute-done.34), channel_id=1, source_target_pairs={{0,15},{1,0},{2,1},{3,2},{4,3},{5,4},{6,5},{7,6},{8,7},{9,8},{10,9... | collective-permute-start | bytes 1544 | tf_op jit(solution)/shard_map/ppermute | solution.py:63
  330.1 5.7 %collective-permute-start.37 = (f32[128,1]{0,1:T(1,128)S(1)}, f32[128,1]{0,1:T(1,128)S(1)}, u32[]{:S(2)}, u32[]{:S(2)}) collective-permute-start(f32[128,1]{0,1:T(1,128)S(1)} %collective-permute-done.35), channel_id=1, source_target_pairs={{0,1},{1,2},{2,3},{3,4},{4,5},{5,6},{6,7},{7,8},{8,9},{9,10},{10,1... | collective-permute-start | bytes 1544 | tf_op jit(solution)/shard_map/ppermute | solution.py:60
  330.2 6.5 %collective-permute-start.38 = (f32[128,1]{0,1:T(1,128)S(1)}, f32[128,1]{0,1:T(1,128)S(1)}, u32[]{:S(2)}, u32[]{:S(2)}) collective-permute-start(f32[128,1]{0,1:T(1,128)S(1)} %collective-permute-done.36), channel_id=1, source_target_pairs={{0,15},{1,0},{2,1},{3,2},{4,3},{5,4},{6,5},{7,6},{8,7},{9,8},{10,9... | collective-permute-start | bytes 1544 | tf_op jit(solution)/shard_map/ppermute | solution.py:63
  335.8 5.7 %collective-permute-start.39 = (f32[128,1]{0,1:T(1,128)S(1)}, f32[128,1]{0,1:T(1,128)S(1)}, u32[]{:S(2)}, u32[]{:S(2)}) collective-permute-start(f32[128,1]{0,1:T(1,128)S(1)} %collective-permute-done.37), channel_id=1, source_target_pairs={{0,1},{1,2},{2,3},{3,4},{4,5},{5,6},{6,7},{7,8},{8,9},{9,10},{10,1... | collective-permute-start | bytes 1544 | tf_op jit(solution)/shard_map/ppermute | solution.py:60
  336.7 5.8 %collective-permute-start.40 = (f32[128,1]{0,1:T(1,128)S(1)}, f32[128,1]{0,1:T(1,128)S(1)}, u32[]{:S(2)}, u32[]{:S(2)}) collective-permute-start(f32[128,1]{0,1:T(1,128)S(1)} %collective-permute-done.38), channel_id=1, source_target_pairs={{0,15},{1,0},{2,1},{3,2},{4,3},{5,4},{6,5},{7,6},{8,7},{9,8},{10,9... | collective-permute-start | bytes 1544 | tf_op jit(solution)/shard_map/ppermute | solution.py:63
  341.5 5.7 %collective-permute-start.41 = (f32[128,1]{0,1:T(1,128)S(1)}, f32[128,1]{0,1:T(1,128)S(1)}, u32[]{:S(2)}, u32[]{:S(2)}) collective-permute-start(f32[128,1]{0,1:T(1,128)S(1)} %collective-permute-done.39), channel_id=1, source_target_pairs={{0,1},{1,2},{2,3},{3,4},{4,5},{5,6},{6,7},{7,8},{8,9},{9,10},{10,1... | collective-permute-start | bytes 1544 | tf_op jit(solution)/shard_map/ppermute | solution.py:60
  352.0 30.6 %copy-start.9 = (f32[1792]{0:T(1024)S(1)}, f32[1792]{0:T(1024)}, u32[]{:S(2)}) copy-start(f32[1792]{0:T(1024)} %param.9) | copy-start | bytes 21508
  352.0 5.2 %collective-permute-start.26 = (bf16[128,128]{1,0:T(8,128)(2,1)S(1)}, bf16[128,128]{1,0:T(8,128)(2,1)S(1)}, u32[]{:S(2)}, u32[]{:S(2)}) collective-permute-start(bf16[128,128]{1,0:T(8,128)(2,1)S(1)} %get-tuple-element.33), channel_id=1, source_target_pairs={{1,0},{2,1},{3,2},{4,3},{5,4},{6,5},{7,6},{8,7},{9,8},{10,9},{11,1... | collective-permute-start | bytes 98312 | tf_op jit(solution)/shard_map/ppermute | solution.py:19
  353.3 3.9 collective-permute-start.25
  357.4 4.6 %collective-permute-start.43 = (f32[128,128]{1,0:T(8,128)S(1)}, f32[128,128]{1,0:T(8,128)S(1)}, u32[]{:S(2)}, u32[]{:S(2)}) collective-permute-start(f32[128,128]{1,0:T(8,128)S(1)} %get-tuple-element.25), channel_id=1, source_target_pairs={{1,0},{2,1},{3,2},{4,3},{5,4},{6,5},{7,6},{8,7},{9,8},{10,9},{11,1... | collective-permute-start | bytes 196616 | tf_op jit(solution)/shard_map/ppermute | solution.py:19
  358.7 3.9 collective-permute-start.42
  375.4 6.3 %collective-permute-start.45 = (bf16[128,128]{1,0:T(8,128)(2,1)S(1)}, bf16[128,128]{1,0:T(8,128)(2,1)S(1)}, u32[]{:S(2)}, u32[]{:S(2)}) collective-permute-start(bf16[128,128]{1,0:T(8,128)(2,1)S(1)} %get-tuple-element.31), channel_id=1, source_target_pairs={{1,0},{2,1},{3,2},{4,3},{5,4},{6,5},{7,6},{8,7},{9,8},{10,9},{11,1... | collective-permute-start | bytes 98312 | tf_op jit(solution)/shard_map/ppermute | solution.py:19
  376.7 5.8 %collective-permute-start.44 = (bf16[128,128]{1,0:T(8,128)(2,1)S(1)}, bf16[128,128]{1,0:T(8,128)(2,1)S(1)}, u32[]{:S(2)}, u32[]{:S(2)}) collective-permute-start(bf16[128,128]{1,0:T(8,128)(2,1)S(1)} %get-tuple-element.30), channel_id=1, source_target_pairs={{0,1},{1,2},{2,3},{3,4},{4,5},{5,6},{6,7},{7,8},{8,9},{9,10},{10,1... | collective-permute-start | bytes 98312 | tf_op jit(solution)/shard_map/ppermute | solution.py:16
  381.7 0.9 copy-start.2
  382.5 0.6 copy-start.5
  382.5 0.6 copy-start.6
